TPU v7x, 32 devices: a whole 2x2x4 slice. The times are simulated.
32 devices in a mesh: dom: 8 (over y, x, core), sec: 4 (over z).
Axes of the slice: x: 2, y: 2, z: 4, core: 2. Of those that a mesh axis runs over, the one named last changes fastest.
Arguments:
- wavefunction: bfloat16 [8, 8, 4, 128, 128], P('dom', 'sec'), may hold values from -6 to 6
- left_env: bfloat16 [8, 26, 8, 128, 128], P('dom', None, 'sec'), may hold values from -0.109375 to 0.109375
- right_env: bfloat16 [8, 26, 8, 128, 128], P('dom', None, 'sec'), may hold values from -0.5 to 0.5
- local_ops: bfloat16 [26, 4, 4], replicated, may hold values from -3 to 3
- targets: int32 [26, 8], replicated, may hold values from 0 to 7, as said below
Outputs:
- applied: bfloat16 [8, 8, 4, 128, 128], P('dom', 'sec')
Inputs may be any that keep to these rules, and one draw needn't show every extreme that they name: Sector labels are periodic: targets[w,s] is s, (s + 1) mod 8, (s - 1) mod 8 or (s + 4) mod 8; the first MPO index keeps every sector (targets[0,s] = s) and the second moves every sector by 4.
All inputs are finite; a program needn't handle non-finite values.
Results may differ from a plain program's by a relative error of at most 0.01.
Values may be sent and summed in bfloat16 or wider, within the bound.
A program may use at most 128 MiB of HBM per device.

v0:
```python
import functools

import jax
import jax.numpy as jnp
from jax import lax
from jax.experimental import pallas as pl
from jax.experimental.pallas import tpu as pltpu
from jax.sharding import PartitionSpec as P

REACH = 1
MESH = pl.DeviceIdType.MESH
F32 = jnp.float32
BF16 = jnp.bfloat16
FIRST_CUTS = (0, 4, 8)
LAST_CUTS = (0, 2, 4, 6, 8)


def plan(sec, terms, block):
    half = ((terms + 1) // 2 + 1) // 2 * 2
    pieces = [(0, half), (half, terms)]
    chunks = []
    for s in range(sec):
        cuts = FIRST_CUTS if s < sec - 1 else LAST_CUTS
        cuts = [block * cut // 8 for cut in cuts]
        chunks += [(s, d0, d1) for d0, d1 in zip(cuts, cuts[1:])]
    return chunks, pieces


def kernel(
    all_sectors, ops_hbm, tgt_hbm, psi_hbm, left_ref, right_ref, out_ref,
    ops_ref, tgt_ref, psi_ref, table, marks, lbuf, rbuf, psit, lpt, rm, acc, mid, low_out, high_out, far_out, low_in, high_in, far_in,
    isem, lsem, rsend, rrecv, zsend, zrecv,
):
    _, sec, phys, block, _ = psi_hbm.shape
    terms = left_ref.shape[1]
    chunks, pieces = plan(sec, terms, block)
    n_dom, n_sec = lax.axis_size("dom"), lax.axis_size("sec")
    dom, col = lax.axis_index("dom"), lax.axis_index("sec")
    before, after = lax.rem(dom + n_dom - 1, n_dom), lax.rem(dom + 1, n_dom)
    below, above = lax.rem(col + n_sec - 1, n_sec), lax.rem(col + 1, n_sec)
    across = lax.rem(col + n_sec // 2, n_sec)
    first = col * sec

    barrier = pltpu.get_barrier_semaphore()
    for where in ({"dom": before}, {"dom": after}, {"sec": below}, {"sec": above}, {"sec": across}):
        pl.semaphore_signal(barrier, inc=1, device_id=where, device_id_type=MESH)

    small_copies = [
        pltpu.make_async_copy(psi_hbm, psi_ref, isem.at[0]),
        pltpu.make_async_copy(ops_hbm, ops_ref, isem.at[1]),
        pltpu.make_async_copy(tgt_hbm, tgt_ref, isem.at[2]),
    ]
    for copy in small_copies:
        copy.start()
    left_copies = [
        pltpu.make_async_copy(left_ref.at[0, :, s], lbuf.at[s], lsem.at[s]) for s in range(sec)
    ]
    for copy in left_copies:
        copy.start()

    pl.semaphore_wait(barrier, 5)

    right_copies = []
    for c, (s, d0, d1) in enumerate(chunks):
        row = []
        for p, (w0, w1) in enumerate(pieces):
            row.append(
                pltpu.make_async_remote_copy(
                    src_ref=right_ref.at[0, pl.ds(w0, w1 - w0), s, pl.ds(d0, d1 - d0)],
                    dst_ref=rbuf.at[s, pl.ds(w0, w1 - w0), pl.ds(d0, d1 - d0)],
                    send_sem=rsend.at[c, p],
                    recv_sem=rrecv.at[c, p],
                    device_id={"dom": before},
                    device_id_type=MESH,
                )
            )
            row[-1].start()
        right_copies.append(row)

    for copy in small_copies:
        copy.wait()
    for i in range(phys):
        row = ops_ref[i].astype(F32)
        for w in range(terms):
            table[w, i] = jnp.broadcast_to(row[:, w : w + 1], (phys, block))
    for s in range(sec):
        for w in range(terms):
            goal = tgt_ref[first + s, w]
            for k, step in enumerate((-REACH, 0, REACH, all_sectors // 2)):
                want = lax.rem(first + s + step + all_sectors, all_sectors)
                marks[s, w, k] = jnp.full((16, block), (goal == want).astype(F32)).astype(BF16)
    for s in range(sec):
        for q in range(phys):
            psit[s, q * block : (q + 1) * block, :] = psi_ref[0, s, q].astype(F32).T.astype(BF16)

    def contract_left(s):
        left_copies[s].wait()

        def left_group(w0, count):
            for v in range(0, count, 2):
                pair = lbuf[s, pl.ds(w0 + v, 2)].reshape(2 * block, block)
                z = lax.dot_general(
                    psit[s], pair, (((1,), (1,)), ((), ())), preferred_element_type=F32
                ).astype(BF16)
                for u in range(2):
                    w = w0 + v + u
                    rows = pl.ds(pl.multiple_of(w * block, block), block)
                    piece = [
                        z[q * block : (q + 1) * block, u * block : (u + 1) * block].reshape(
                            block // 16, 16, block
                        )
                        for q in range(phys)
                    ]
                    for i in range(phys):
                        total = None
                        for q in range(phys):
                            factor = jnp.broadcast_to(table[w, i, q : q + 1, :], (16, block))
                            part = factor.astype(BF16)[None] * piece[q]
                            total = part if total is None else total + part
                        lpt[s, rows, i * block : (i + 1) * block] = total.reshape(block, block)

        def left_quad(j, carry):
            left_group(4 * j, 4)
            return carry

        lax.fori_loop(0, terms // 4, left_quad, 0)
        if terms % 4:
            left_group(terms // 4 * 4, terms % 4)

    contract_left(0)

    def z_copy(m, src, dst, where):
        return pltpu.make_async_remote_copy(
            src_ref=src, dst_ref=dst, send_sem=zsend.at[m], recv_sem=zrecv.at[m],
            device_id={"sec": where}, device_id_type=MESH,
        )

    z_sent = []
    z_due = []
    n_msg = 0
    for c, (s, d0, d1) in enumerate(chunks):
        size = d1 - d0
        for p, (w0, w1) in enumerate(pieces):
            right_copies[c][p].wait_recv()

            for w in range(w0, w1):
                right = rbuf[s, w, pl.ds(d0, size)].reshape(size // 16, 16, block)
                column = slice((w - w0) * block, (w - w0 + 1) * block)
                for k in range(4):
                    rm[k * size : (k + 1) * size, column] = (
                        right * marks[s, w, k][None]
                    ).reshape(size, block)
            part = jnp.dot(
                rm[: 4 * size, : (w1 - w0) * block],
                lpt[s, w0 * block : w1 * block, :],
                preferred_element_type=F32,
            )
            if p == 0:
                acc[: 4 * size, :] = part
            else:
                acc[: 4 * size, :] += part
        sums = [acc[k * size : (k + 1) * size, :] for k in range(4)]
        ds = pl.ds(d0, size)
        due = []
        far_out[s, ds] = sums[3].astype(BF16)
        due.append(z_copy(n_msg, far_out.at[s, ds], far_in.at[s, ds], across))
        n_msg += 1
        if s == 0:
            low_out[ds] = sums[0].astype(BF16)
            due.append(z_copy(n_msg, low_out.at[ds], low_in.at[ds], below))
            n_msg += 1
        if s == sec - 1:
            high_out[ds] = sums[2].astype(BF16)
            due.append(z_copy(n_msg, high_out.at[ds], high_in.at[ds], above))
            n_msg += 1
        for copy in due:
            copy.start()
        z_sent += due
        if s < sec - 1 and d0 == 0:
            contract_left(s + 1)
        if s > 0:
            mid[s - 1, ds] += sums[0]
            mid[s, ds] += sums[1]
        else:
            mid[s, ds] = sums[1]
        if s < sec - 1:
            mid[s + 1, ds] = sums[2]
            for copy in due:
                z_due.append(copy)
        else:
            z_due.append((d0, d1, due))

    for entry in z_due:
        if not isinstance(entry, tuple):
            entry.wait_recv()
            continue
        d0, d1, due = entry
        for copy in due:
            copy.wait_recv()
        ds = pl.ds(d0, d1 - d0)
        for t in range(sec):
            total = mid[t, ds] + far_in[t, ds].astype(F32)
            if t == 0:
                total = total + high_in[ds].astype(F32)
            if t == sec - 1:
                total = total + low_in[ds].astype(F32)
            for i in range(phys):
                out_ref[0, t, i, :, d0:d1] = total[:, i * block : (i + 1) * block].T.astype(BF16)
    for row in right_copies:
        for copy in row:
            copy.wait_send()
    for copy in z_sent:
        copy.wait_send()


def local(wavefunction, left_env, right_env, local_ops, targets):
    _, sec, phys, block, _ = wavefunction.shape
    terms = left_env.shape[1]
    wide = phys * block
    chunks, pieces = plan(sec, terms, block)
    n_msg = sum(1 + (s == 0) + (s == sec - 1) for s, _, _ in chunks)
    longest = max(w1 - w0 for w0, w1 in pieces)
    return pl.pallas_call(
        functools.partial(kernel, targets.shape[1]),
        out_shape=pltpu.VMEM(wavefunction.shape, BF16),
        in_specs=[
            pl.BlockSpec(memory_space=pl.ANY),
            pl.BlockSpec(memory_space=pl.ANY),
            pl.BlockSpec(memory_space=pl.ANY),
            pl.BlockSpec(memory_space=pl.ANY),
            pl.BlockSpec(memory_space=pl.ANY),
        ],
        out_specs=pl.BlockSpec(memory_space=pltpu.VMEM),
        scratch_shapes=[
            pltpu.VMEM((phys, phys, terms), BF16),
            pltpu.SMEM(targets.shape[::-1], jnp.int32),
            pltpu.VMEM(wavefunction.shape, BF16),
            pltpu.VMEM((terms, phys, phys, block), F32),
            pltpu.VMEM((sec, terms, 4, 16, block), BF16),
            pltpu.VMEM((sec, terms, block, block), BF16),
            pltpu.VMEM((sec, terms, block, block), BF16),
            pltpu.VMEM((sec, wide, block), BF16),
            pltpu.VMEM((sec, terms * block, wide), BF16),
            pltpu.VMEM((4 * block, longest * block), BF16),
            pltpu.VMEM((4 * block, wide), F32),
            pltpu.VMEM((sec, block, wide), F32),
            pltpu.VMEM((block, wide), BF16),
            pltpu.VMEM((block, wide), BF16),
            pltpu.VMEM((sec, block, wide), BF16),
            pltpu.VMEM((block, wide), BF16),
            pltpu.VMEM((block, wide), BF16),
            pltpu.VMEM((sec, block, wide), BF16),
            pltpu.SemaphoreType.DMA((3,)),
            pltpu.SemaphoreType.DMA((sec,)),
            pltpu.SemaphoreType.DMA((len(chunks), len(pieces))),
            pltpu.SemaphoreType.DMA((len(chunks), len(pieces))),
            pltpu.SemaphoreType.DMA((n_msg,)),
            pltpu.SemaphoreType.DMA((n_msg,)),
        ],
        compiler_params=pltpu.CompilerParams(collective_id=0, has_side_effects=True),
    )(local_ops.transpose(1, 2, 0), targets.T, wavefunction, left_env, right_env)


def solution(mesh):
    return jax.shard_map(
        local,
        mesh=mesh,
        in_specs=(
            P("dom", "sec", None, None, None),
            P("dom", None, "sec", None, None),
            P("dom", None, "sec", None, None),
            P(),
            P(),
        ),
        out_specs=P("dom", "sec", None, None, None),
        check_vma=False,
    )
```

profile of v0, /device:TPU:1, one launch (start us, length us, event | category | flops | bytes accessed | tf_op | source)
XLA Modules:
  0.0 30.3 jit_solution(5376941283952047578)
XLA Ops:
  0.0 29.6 %shard_map.55 = bf16[1,2,4,128,128]{4,3,2,1,0:T(8,128)(2,1)S(1)} custom-call(bf16[4,4,26]{2,1,0:T(4,128)(2,1)} %bitcast.2, s32[8,26]{1,0:T(8,128)} %bitcast.3, bf16[1,2,4,128,128]{4,3,2,1,0:T(8,128)(2,1)} %psi_hbm.1, bf16[1,26,2,128,128]{4,3,2,1,0:T(8,128)(2,1)} %left_ref.1, bf16[1,26,2,128,128]{4,3,2,1,0:T(8,128)(2,1)} %right_ref.1), custom_call_target="tpu_custom_call" | custom-call | tf_op jit(solution)/shard_map/pallas_call | solution.py:223
  29.6 0.7 %copy.7 = bf16[1,2,4,128,128]{4,3,2,1,0:T(8,128)(2,1)} copy(bf16[1,2,4,128,128]{4,3,2,1,0:T(8,128)(2,1)S(1)} %shard_map.55) | data formatting | bytes 524288
where the time goes:
time: 30.4 us; the launch traced here: 30.3 us
  Pallas kernels  29.6 us (97%)
  local copies, waits for them, and re-layouts  0.71 us (2%)
    pallas_call x1, Pallas kernels, local(): pl.pallas_call(functools.partial(kernel, targets.shape[1]), out_shape=plt...  29.6 us
    unnamed x1, local copies, waits for them, and re-layouts  0.71 us

commit v1 on v0

--- a/solution.py
+++ b/solution.py
@@ -13,23 +13,28 @@
 BF16 = jnp.bfloat16
 FIRST_CUTS = (0, 4, 8)
 LAST_CUTS = (0, 2, 4, 6, 8)
+PIECES = 2
 
 
 def plan(sec, terms, block):
-    half = ((terms + 1) // 2 + 1) // 2 * 2
-    pieces = [(0, half), (half, terms)]
+    edges = [1 + (terms - 1) * p // PIECES for p in range(PIECES + 1)]
+    pieces = list(zip(edges, edges[1:]))
     chunks = []
-    for s in range(sec):
-        cuts = FIRST_CUTS if s < sec - 1 else LAST_CUTS
+    for s in reversed(range(sec)):
+        cuts = LAST_CUTS if s == 0 else FIRST_CUTS
         cuts = [block * cut // 8 for cut in cuts]
         chunks += [(s, d0, d1) for d0, d1 in zip(cuts, cuts[1:])]
     return chunks, pieces
 
 
+def joins(n_sec, sec):
+    return n_sec == 4 and sec > 1
+
+
 def kernel(
     all_sectors, ops_hbm, tgt_hbm, psi_hbm, left_ref, right_ref, out_ref,
-    ops_ref, tgt_ref, psi_ref, table, marks, lbuf, rbuf, psit, lpt, rm, acc, mid, low_out, high_out, far_out, low_in, high_in, far_in,
-    isem, lsem, rsend, rrecv, zsend, zrecv,
+    ops_ref, tgt_ref, psi_ref, table, marks, lbuf, rbuf, psit, lpt, rm, acc, mid, low_out, high_out, far_out, low_in, high_in, far_in, via_in,
+    isem, lsem, rsend, rrecv, ksend, krecv, zsend, zrecv, vrecv, ready,
 ):
     _, sec, phys, block, _ = psi_hbm.shape
     terms = left_ref.shape[1]
@@ -39,11 +44,41 @@
     before, after = lax.rem(dom + n_dom - 1, n_dom), lax.rem(dom + 1, n_dom)
     below, above = lax.rem(col + n_sec - 1, n_sec), lax.rem(col + 1, n_sec)
     across = lax.rem(col + n_sec // 2, n_sec)
+    peers = (below, above, across)
     first = col * sec
+    relay = joins(n_sec, sec)
+    low_end, low_mid = col == 0, col == 1
+    high_mid, high_end = col == n_sec - 2, col == n_sec - 1
 
     barrier = pltpu.get_barrier_semaphore()
-    for where in ({"dom": before}, {"dom": after}, {"sec": below}, {"sec": above}, {"sec": across}):
-        pl.semaphore_signal(barrier, inc=1, device_id=where, device_id_type=MESH)
+    pl.semaphore_signal(barrier, inc=1, device_id={"dom": after}, device_id_type=MESH)
+    lower = jnp.int32(0)
+    for peer in peers:
+        lower += (peer < col).astype(jnp.int32)
+
+        @pl.when(peer > col)
+        def _():
+            pl.semaphore_signal(barrier, inc=1, device_id={"sec": peer}, device_id_type=MESH)
+
+    pl.semaphore_wait(barrier, 1 + lower)
+
+    def r_copy(src, dst, send, recv):
+        return pltpu.make_async_remote_copy(
+            src_ref=src, dst_ref=dst, send_sem=send, recv_sem=recv, device_id={"dom": before}, device_id_type=MESH,
+        )
+
+    right_copies = []
+    for c, (s, d0, d1) in enumerate(chunks):
+        row = []
+        for p, (w0, w1) in enumerate(pieces):
+            ws, ds = pl.ds(w0, w1 - w0), pl.ds(d0, d1 - d0)
+            row.append(r_copy(right_ref.at[0, ws, s, ds], rbuf.at[s, ws, ds], rsend.at[c, p], rrecv.at[c, p]))
+            row[-1].start()
+        right_copies.append(row)
+    keep_copies = []
+    for s in range(sec):
+        keep_copies.append(r_copy(right_ref.at[0, 0, s], rbuf.at[s, 0], ksend.at[s], krecv.at[s]))
+        keep_copies[-1].start()
 
     small_copies = [
         pltpu.make_async_copy(psi_hbm, psi_ref, isem.at[0]),
@@ -52,30 +87,15 @@
     ]
     for copy in small_copies:
         copy.start()
-    left_copies = [
-        pltpu.make_async_copy(left_ref.at[0, :, s], lbuf.at[s], lsem.at[s]) for s in range(sec)
-    ]
-    for copy in left_copies:
+    left_copies = [pltpu.make_async_copy(left_ref.at[0, :, s], lbuf.at[s], lsem.at[s]) for s in range(sec)]
+    for copy in reversed(left_copies):
         copy.start()
 
-    pl.semaphore_wait(barrier, 5)
-
-    right_copies = []
-    for c, (s, d0, d1) in enumerate(chunks):
-        row = []
-        for p, (w0, w1) in enumerate(pieces):
-            row.append(
-                pltpu.make_async_remote_copy(
-                    src_ref=right_ref.at[0, pl.ds(w0, w1 - w0), s, pl.ds(d0, d1 - d0)],
-                    dst_ref=rbuf.at[s, pl.ds(w0, w1 - w0), pl.ds(d0, d1 - d0)],
-                    send_sem=rsend.at[c, p],
-                    recv_sem=rrecv.at[c, p],
-                    device_id={"dom": before},
-                    device_id_type=MESH,
-                )
-            )
-            row[-1].start()
-        right_copies.append(row)
+    for peer in peers:
+
+        @pl.when(peer < col)
+        def _():
+            pl.semaphore_signal(ready, inc=1, device_id={"sec": peer}, device_id_type=MESH)
 
     for copy in small_copies:
         copy.wait()
@@ -84,7 +104,7 @@
         for w in range(terms):
             table[w, i] = jnp.broadcast_to(row[:, w : w + 1], (phys, block))
     for s in range(sec):
-        for w in range(terms):
+        for w in range(1, terms):
             goal = tgt_ref[first + s, w]
             for k, step in enumerate((-REACH, 0, REACH, all_sectors // 2)):
                 want = lax.rem(first + s + step + all_sectors, all_sectors)
@@ -127,22 +147,74 @@
         if terms % 4:
             left_group(terms // 4 * 4, terms % 4)
 
-    contract_left(0)
-
-    def z_copy(m, src, dst, where):
+    contract_left(sec - 1)
+    @pl.when(lower < len(peers))
+    def _():
+        pl.semaphore_wait(ready, len(peers) - lower)
+
+
+    def z_copy(m, src, dst, where, arrived=None):
         return pltpu.make_async_remote_copy(
-            src_ref=src, dst_ref=dst, send_sem=zsend.at[m], recv_sem=zrecv.at[m],
+            src_ref=src, dst_ref=dst, send_sem=zsend.at[m], recv_sem=(zrecv if arrived is None else arrived).at[m],
             device_id={"sec": where}, device_id_type=MESH,
         )
 
+    def only(condition, action):
+        if condition is True:
+            action()
+        elif condition is not False:
+            pl.when(condition)(action)
+
+    if relay:
+        for mine, landing in (
+            (low_end, high_in), (low_mid, far_in.at[sec - 1]), (high_mid, far_in.at[0]), (high_end, low_in),
+        ):
+
+            @pl.when(mine)
+            def _():
+                landing[...] = jnp.zeros_like(landing)
+
     z_sent = []
     z_due = []
+    via_due = []
+    keep_rows = []
     n_msg = 0
+
+    def settle(due, d0, d1, here=False):
+        rest = []
+        for entry in due:
+            if entry[1] < d1 and d0 < entry[2]:
+                only(True if here else entry[0], entry[3].wait_recv)
+            else:
+                rest.append(entry)
+        return rest
+
+    def send_on(d0, d1):
+        ds = pl.ds(d0, d1 - d0)
+        moves = [
+            (via_in.at[0, ds], high_out.at[ds], high_in.at[ds], above),
+            (via_in.at[1, ds], far_out.at[sec - 1, ds], far_in.at[sec - 1, ds], across),
+        ]
+        copies = [z_copy(n_msg + j, held, landing, where) for j, (_, held, landing, where) in enumerate(moves)]
+
+        @pl.when(low_mid)
+        def _():
+            settle(via_up, d0, d1, here=True)
+            for (via, held, _, _), copy in zip(moves, copies):
+                held[...] = (held[...].astype(F32) + via[...].astype(F32)).astype(BF16)
+                copy.start()
+
+        via_up[:] = [entry for entry in via_up if not (entry[1] < d1 and d0 < entry[2])]
+        for copy, receiver in zip(copies, (high_mid, high_end)):
+            z_sent.append((low_mid, copy))
+            z_due.append((receiver, d0, d1, copy))
+
+    via_up = []
+    to_send_on = []
     for c, (s, d0, d1) in enumerate(chunks):
         size = d1 - d0
         for p, (w0, w1) in enumerate(pieces):
             right_copies[c][p].wait_recv()
-
             for w in range(w0, w1):
                 right = rbuf[s, w, pl.ds(d0, size)].reshape(size // 16, 16, block)
                 column = slice((w - w0) * block, (w - w0 + 1) * block)
@@ -161,42 +233,81 @@
                 acc[: 4 * size, :] += part
         sums = [acc[k * size : (k + 1) * size, :] for k in range(4)]
         ds = pl.ds(d0, size)
-        due = []
-        far_out[s, ds] = sums[3].astype(BF16)
-        due.append(z_copy(n_msg, far_out.at[s, ds], far_in.at[s, ds], across))
-        n_msg += 1
-        if s == 0:
-            low_out[ds] = sums[0].astype(BF16)
-            due.append(z_copy(n_msg, low_out.at[ds], low_in.at[ds], below))
-            n_msg += 1
+        if relay and s == 0:
+
+            @pl.when(high_mid)
+            def _():
+                settle(via_due, d0, d1, here=True)
+                far_out[s, ds] = (sums[3] + via_in[1, ds].astype(F32)).astype(BF16)
+                low_out[ds] = (sums[0] + via_in[0, ds].astype(F32)).astype(BF16)
+
+            @pl.when(col != n_sec - 2)
+            def _():
+                far_out[s, ds] = sums[3].astype(BF16)
+                low_out[ds] = sums[0].astype(BF16)
+
+            via_due = [entry for entry in via_due if not (entry[1] < d1 and d0 < entry[2])]
+        else:
+            far_out[s, ds] = sums[3].astype(BF16)
+            if s == 0:
+                low_out[ds] = sums[0].astype(BF16)
         if s == sec - 1:
             high_out[ds] = sums[2].astype(BF16)
-            due.append(z_copy(n_msg, high_out.at[ds], high_in.at[ds], above))
+
+        messages = [("far", far_out.at[s, ds], far_in.at[s, ds], across)]
+        if s == 0:
+            messages.append(("low", low_out.at[ds], low_in.at[ds], below))
+        if s == sec - 1:
+            messages.append(("high", high_out.at[ds], high_in.at[ds], above))
+        for kind, src, landing, where in messages:
+            copy = z_copy(n_msg, src, landing, where)
+            straight, due = True, True
+            if relay and s in (0, sec - 1):
+                rising = s == 0
+                end, mid_col = (low_end, low_mid) if rising else (high_end, high_mid)
+                step = above if rising else below
+                via = z_copy(n_msg, src, via_in.at[0 if kind == "far" else 1, ds], step, vrecv)
+                only(end, via.start)
+                (via_up if rising else via_due).append((mid_col, d0, d1, via))
+                if rising:
+                    straight = col != 0
+                    due = (col != n_sec - 2) if kind == "far" else (col != n_sec - 1)
+                    z_sent.append((True, copy))
+                else:
+                    straight = jnp.logical_and(col != 1, col != n_sec - 1)
+                    due = lax.rem(col, 2) == 0 if kind == "far" else lax.rem(col, 2) == 1
+                    z_sent.append((col != 1, copy))
+            else:
+                z_sent.append((True, copy))
+            only(straight, copy.start)
+            z_due.append((due, d0, d1, copy))
             n_msg += 1
-        for copy in due:
-            copy.start()
-        z_sent += due
-        if s < sec - 1 and d0 == 0:
-            contract_left(s + 1)
-        if s > 0:
-            mid[s - 1, ds] += sums[0]
+        if relay and s == 0:
+            to_send_on.append((d0, d1))
+            if len(to_send_on) > 1:
+                send_on(*to_send_on.pop(0))
+                n_msg += 2
+
+        if s > 0 and d0 == 0:
+            contract_left(s - 1)
+        if s < sec - 1:
+            mid[s + 1, ds] += sums[2]
             mid[s, ds] += sums[1]
         else:
             mid[s, ds] = sums[1]
-        if s < sec - 1:
-            mid[s + 1, ds] = sums[2]
-            for copy in due:
-                z_due.append(copy)
+        if s > 0:
+            mid[s - 1, ds] = sums[0]
         else:
-            z_due.append((d0, d1, due))
-
-    for entry in z_due:
-        if not isinstance(entry, tuple):
-            entry.wait_recv()
-            continue
-        d0, d1, due = entry
-        for copy in due:
-            copy.wait_recv()
+            keep_rows.append((d0, d1))
+
+    for s in reversed(range(sec)):
+        keep_copies[s].wait_recv()
+        mid[s] += jnp.dot(rbuf[s, 0], lpt[s, :block, :], preferred_element_type=F32)
+    for rows in to_send_on:
+        send_on(*rows)
+        n_msg += 2
+    for d0, d1 in keep_rows:
+        z_due = settle(z_due, d0, d1)
         ds = pl.ds(d0, d1 - d0)
         for t in range(sec):
             total = mid[t, ds] + far_in[t, ds].astype(F32)
@@ -206,11 +317,11 @@
                 total = total + low_in[ds].astype(F32)
             for i in range(phys):
                 out_ref[0, t, i, :, d0:d1] = total[:, i * block : (i + 1) * block].T.astype(BF16)
-    for row in right_copies:
+    for row in right_copies + [keep_copies]:
         for copy in row:
             copy.wait_send()
-    for copy in z_sent:
-        copy.wait_send()
+    for senders, copy in z_sent:
+        only(senders, copy.wait_send)
 
 
 def local(wavefunction, left_env, right_env, local_ops, targets):
@@ -219,6 +330,8 @@
     wide = phys * block
     chunks, pieces = plan(sec, terms, block)
     n_msg = sum(1 + (s == 0) + (s == sec - 1) for s, _, _ in chunks)
+    if joins(lax.axis_size("sec"), sec):
+        n_msg += sum(2 * (s == 0) for s, _, _ in chunks)
     longest = max(w1 - w0 for w0, w1 in pieces)
     return pl.pallas_call(
         functools.partial(kernel, targets.shape[1]),
@@ -250,12 +363,17 @@
             pltpu.VMEM((block, wide), BF16),
             pltpu.VMEM((block, wide), BF16),
             pltpu.VMEM((sec, block, wide), BF16),
+            pltpu.VMEM((2, block, wide), BF16),
             pltpu.SemaphoreType.DMA((3,)),
             pltpu.SemaphoreType.DMA((sec,)),
             pltpu.SemaphoreType.DMA((len(chunks), len(pieces))),
             pltpu.SemaphoreType.DMA((len(chunks), len(pieces))),
+            pltpu.SemaphoreType.DMA((sec,)),
+            pltpu.SemaphoreType.DMA((sec,)),
             pltpu.SemaphoreType.DMA((n_msg,)),
             pltpu.SemaphoreType.DMA((n_msg,)),
+            pltpu.SemaphoreType.DMA((n_msg,)),
+            pltpu.SemaphoreType.REGULAR,
         ],
         compiler_params=pltpu.CompilerParams(collective_id=0, has_side_effects=True),
     )(local_ops.transpose(1, 2, 0), targets.T, wavefunction, left_env, right_env)

time: 30.4 us -> 28.5 us (0.938)
  Pallas kernels: 29.6 us -> 27.6 us
    pallas_call x1, Pallas kernels: 29.6 us -> 27.6 us  [local(): pl.pallas_call(functools.partial(kernel, targets.shape[1]), out_shape=plt...]
where the time goes in v1:
time: 28.5 us; the launch traced here: 28.3 us
  Pallas kernels  27.6 us (97%)
  local copies, waits for them, and re-layouts  0.71 us (2%)
    pallas_call x1, Pallas kernels, local(): pl.pallas_call(functools.partial(kernel, targets.shape[1]), out_shape=plt...  27.6 us
    unnamed x1, local copies, waits for them, and re-layouts  0.71 us

profile of v1, /device:TPU:1, one launch (start us, length us, event | category | flops | bytes accessed | tf_op | source)
XLA Modules:
  0.0 28.3 jit_solution(9861911332761020303)
XLA Ops:
  0.0 27.6 %shard_map.55 = bf16[1,2,4,128,128]{4,3,2,1,0:T(8,128)(2,1)S(1)} custom-call(bf16[4,4,26]{2,1,0:T(4,128)(2,1)} %bitcast.2, s32[8,26]{1,0:T(8,128)} %bitcast.3, bf16[1,2,4,128,128]{4,3,2,1,0:T(8,128)(2,1)} %psi_hbm.1, bf16[1,26,2,128,128]{4,3,2,1,0:T(8,128)(2,1)} %left_ref.1, bf16[1,26,2,128,128]{4,3,2,1,0:T(8,128)(2,1)} %right_ref.1), custom_call_target="tpu_custom_call" | custom-call | tf_op jit(solution)/shard_map/pallas_call | solution.py:336
  27.6 0.7 %copy.7 = bf16[1,2,4,128,128]{4,3,2,1,0:T(8,128)(2,1)} copy(bf16[1,2,4,128,128]{4,3,2,1,0:T(8,128)(2,1)S(1)} %shard_map.55) | data formatting | bytes 524288

commit v2 on v1

--- a/solution.py
+++ b/solution.py
@@ -12,18 +12,18 @@
 F32 = jnp.float32
 BF16 = jnp.bfloat16
 FIRST_CUTS = (0, 4, 8)
-LAST_CUTS = (0, 2, 4, 6, 8)
-PIECES = 2
+LAST_CUTS = (0, 4, 6, 7, 8)
+PIECES = (3, 5)
 
 
 def plan(sec, terms, block):
-    edges = [1 + (terms - 1) * p // PIECES for p in range(PIECES + 1)]
-    pieces = list(zip(edges, edges[1:]))
     chunks = []
     for s in reversed(range(sec)):
         cuts = LAST_CUTS if s == 0 else FIRST_CUTS
         cuts = [block * cut // 8 for cut in cuts]
         chunks += [(s, d0, d1) for d0, d1 in zip(cuts, cuts[1:])]
+    edges = [1 + (terms - 1) * cut // PIECES[-1] for cut in (0,) + PIECES]
+    pieces = [[(1, terms)] for _ in chunks[1:]] + [list(zip(edges, edges[1:]))]
     return chunks, pieces
 
 
@@ -33,7 +33,7 @@
 
 def kernel(
     all_sectors, ops_hbm, tgt_hbm, psi_hbm, left_ref, right_ref, out_ref,
-    ops_ref, tgt_ref, psi_ref, table, marks, lbuf, rbuf, psit, lpt, rm, acc, mid, low_out, high_out, far_out, low_in, high_in, far_in, via_in,
+    ops_ref, tgt_ref, psi_ref, table, marks, lbuf, rbuf, psit, lpt, rm, acc, mid, low_out, high_out, far_out, low_in, high_in, far_in, via_in, fin,
     isem, lsem, rsend, rrecv, ksend, krecv, zsend, zrecv, vrecv, ready,
 ):
     _, sec, phys, block, _ = psi_hbm.shape
@@ -60,26 +60,6 @@
         def _():
             pl.semaphore_signal(barrier, inc=1, device_id={"sec": peer}, device_id_type=MESH)
 
-    pl.semaphore_wait(barrier, 1 + lower)
-
-    def r_copy(src, dst, send, recv):
-        return pltpu.make_async_remote_copy(
-            src_ref=src, dst_ref=dst, send_sem=send, recv_sem=recv, device_id={"dom": before}, device_id_type=MESH,
-        )
-
-    right_copies = []
-    for c, (s, d0, d1) in enumerate(chunks):
-        row = []
-        for p, (w0, w1) in enumerate(pieces):
-            ws, ds = pl.ds(w0, w1 - w0), pl.ds(d0, d1 - d0)
-            row.append(r_copy(right_ref.at[0, ws, s, ds], rbuf.at[s, ws, ds], rsend.at[c, p], rrecv.at[c, p]))
-            row[-1].start()
-        right_copies.append(row)
-    keep_copies = []
-    for s in range(sec):
-        keep_copies.append(r_copy(right_ref.at[0, 0, s], rbuf.at[s, 0], ksend.at[s], krecv.at[s]))
-        keep_copies[-1].start()
-
     small_copies = [
         pltpu.make_async_copy(psi_hbm, psi_ref, isem.at[0]),
         pltpu.make_async_copy(ops_hbm, ops_ref, isem.at[1]),
@@ -91,27 +71,51 @@
     for copy in reversed(left_copies):
         copy.start()
 
+    def prepare():
+        for copy in small_copies:
+            copy.wait()
+        for i in range(phys):
+            row = ops_ref[i].astype(F32)
+            for w in range(terms):
+                table[w, i] = jnp.broadcast_to(row[:, w : w + 1], (phys, block))
+        for s in range(sec):
+            for w in range(1, terms):
+                goal = tgt_ref[first + s, w]
+                for k, step in enumerate((-REACH, 0, REACH, all_sectors // 2)):
+                    want = lax.rem(first + s + step + all_sectors, all_sectors)
+                    marks[s, w, k] = jnp.full((16, block), (goal == want).astype(F32)).astype(BF16)
+        for s in range(sec):
+            for q in range(phys):
+                psit[s, q * block : (q + 1) * block, :] = psi_ref[0, s, q].astype(F32).T.astype(BF16)
+
+    pl.when(dom == 0)(prepare)
+    pl.semaphore_wait(barrier, 1 + lower)
+
+    def r_copy(src, dst, send, recv):
+        return pltpu.make_async_remote_copy(
+            src_ref=src, dst_ref=dst, send_sem=send, recv_sem=recv, device_id={"dom": before}, device_id_type=MESH,
+        )
+
+    right_copies = []
+    for c, (s, d0, d1) in enumerate(chunks):
+        row = []
+        for p, (w0, w1) in enumerate(pieces[c]):
+            ws, ds = pl.ds(w0, w1 - w0), pl.ds(d0, d1 - d0)
+            row.append(r_copy(right_ref.at[0, ws, s, ds], rbuf.at[s, ws, ds], rsend.at[c, p], rrecv.at[c, p]))
+            row[-1].start()
+        right_copies.append(row)
+    keep_copies = []
+    for s in range(sec):
+        keep_copies.append(r_copy(right_ref.at[0, 0, s], rbuf.at[s, 0], ksend.at[s], krecv.at[s]))
+        keep_copies[-1].start()
+
     for peer in peers:
 
         @pl.when(peer < col)
         def _():
             pl.semaphore_signal(ready, inc=1, device_id={"sec": peer}, device_id_type=MESH)
 
-    for copy in small_copies:
-        copy.wait()
-    for i in range(phys):
-        row = ops_ref[i].astype(F32)
-        for w in range(terms):
-            table[w, i] = jnp.broadcast_to(row[:, w : w + 1], (phys, block))
-    for s in range(sec):
-        for w in range(1, terms):
-            goal = tgt_ref[first + s, w]
-            for k, step in enumerate((-REACH, 0, REACH, all_sectors // 2)):
-                want = lax.rem(first + s + step + all_sectors, all_sectors)
-                marks[s, w, k] = jnp.full((16, block), (goal == want).astype(F32)).astype(BF16)
-    for s in range(sec):
-        for q in range(phys):
-            psit[s, q * block : (q + 1) * block, :] = psi_ref[0, s, q].astype(F32).T.astype(BF16)
+    pl.when(dom != 0)(prepare)
 
     def contract_left(s):
         left_copies[s].wait()
@@ -213,7 +217,7 @@
     to_send_on = []
     for c, (s, d0, d1) in enumerate(chunks):
         size = d1 - d0
-        for p, (w0, w1) in enumerate(pieces):
+        for p, (w0, w1) in enumerate(pieces[c]):
             right_copies[c][p].wait_recv()
             for w in range(w0, w1):
                 right = rbuf[s, w, pl.ds(d0, size)].reshape(size // 16, 16, block)
@@ -315,8 +319,10 @@
                 total = total + high_in[ds].astype(F32)
             if t == sec - 1:
                 total = total + low_in[ds].astype(F32)
-            for i in range(phys):
-                out_ref[0, t, i, :, d0:d1] = total[:, i * block : (i + 1) * block].T.astype(BF16)
+            fin[t, ds] = total.astype(BF16)
+    for t in range(sec):
+        for i in range(phys):
+            out_ref[0, t, i] = fin[t, :, i * block : (i + 1) * block].T.astype(BF16)
     for row in right_copies + [keep_copies]:
         for copy in row:
             copy.wait_send()
@@ -332,7 +338,7 @@
     n_msg = sum(1 + (s == 0) + (s == sec - 1) for s, _, _ in chunks)
     if joins(lax.axis_size("sec"), sec):
         n_msg += sum(2 * (s == 0) for s, _, _ in chunks)
-    longest = max(w1 - w0 for w0, w1 in pieces)
+    longest = max(w1 - w0 for row in pieces for w0, w1 in row)
     return pl.pallas_call(
         functools.partial(kernel, targets.shape[1]),
         out_shape=pltpu.VMEM(wavefunction.shape, BF16),
@@ -364,10 +370,11 @@
             pltpu.VMEM((block, wide), BF16),
             pltpu.VMEM((sec, block, wide), BF16),
             pltpu.VMEM((2, block, wide), BF16),
+            pltpu.VMEM((sec, block, wide), BF16),
             pltpu.SemaphoreType.DMA((3,)),
             pltpu.SemaphoreType.DMA((sec,)),
-            pltpu.SemaphoreType.DMA((len(chunks), len(pieces))),
-            pltpu.SemaphoreType.DMA((len(chunks), len(pieces))),
+            pltpu.SemaphoreType.DMA((len(chunks), len(PIECES))),
+            pltpu.SemaphoreType.DMA((len(chunks), len(PIECES))),
             pltpu.SemaphoreType.DMA((sec,)),
             pltpu.SemaphoreType.DMA((sec,)),
             pltpu.SemaphoreType.DMA((n_msg,)),

time: 28.5 us -> 27.9 us (0.979)
  Pallas kernels: 27.6 us -> 27.1 us
    pallas_call x1, Pallas kernels: 27.6 us -> 27.1 us  [local(): pl.pallas_call(functools.partial(kernel, targets.shape[1]), out_shape=plt...]
where the time goes in v2:
time: 27.9 us; the launch traced here: 27.8 us
  Pallas kernels  27.1 us (97%)
  local copies, waits for them, and re-layouts  0.71 us (3%)
    pallas_call x1, Pallas kernels, local(): pl.pallas_call(functools.partial(kernel, targets.shape[1]), out_shape=plt...  27.1 us
    unnamed x1, local copies, waits for them, and re-layouts  0.71 us

profile of v2, /device:TPU:1, one launch (start us, length us, event | category | flops | bytes accessed | tf_op | source)
XLA Modules:
  0.0 27.8 jit_solution(6232461371430802115)
XLA Ops:
  0.0 27.1 %shard_map.55 = bf16[1,2,4,128,128]{4,3,2,1,0:T(8,128)(2,1)S(1)} custom-call(bf16[4,4,26]{2,1,0:T(4,128)(2,1)} %bitcast.2, s32[8,26]{1,0:T(8,128)} %bitcast.3, bf16[1,2,4,128,128]{4,3,2,1,0:T(8,128)(2,1)} %psi_hbm.1, bf16[1,26,2,128,128]{4,3,2,1,0:T(8,128)(2,1)} %left_ref.1, bf16[1,26,2,128,128]{4,3,2,1,0:T(8,128)(2,1)} %right_ref.1), custom_call_target="tpu_custom_call" | custom-call | tf_op jit(solution)/shard_map/pallas_call | solution.py:342
  27.1 0.7 %copy.7 = bf16[1,2,4,128,128]{4,3,2,1,0:T(8,128)(2,1)} copy(bf16[1,2,4,128,128]{4,3,2,1,0:T(8,128)(2,1)S(1)} %shard_map.55) | data formatting | bytes 524288

commit v3 on v2

--- a/solution.py
+++ b/solution.py
@@ -311,6 +311,12 @@
         send_on(*rows)
         n_msg += 2
     for d0, d1 in keep_rows:
+        if d1 == block:
+            for row in right_copies + [keep_copies]:
+                for copy in row:
+                    copy.wait_send()
+            for senders, copy in z_sent:
+                only(senders, copy.wait_send)
         z_due = settle(z_due, d0, d1)
         ds = pl.ds(d0, d1 - d0)
         for t in range(sec):
@@ -323,11 +329,6 @@
     for t in range(sec):
         for i in range(phys):
             out_ref[0, t, i] = fin[t, :, i * block : (i + 1) * block].T.astype(BF16)
-    for row in right_copies + [keep_copies]:
-        for copy in row:
-            copy.wait_send()
-    for senders, copy in z_sent:
-        only(senders, copy.wait_send)
 
 
 def local(wavefunction, left_env, right_env, local_ops, targets):

time: 27.9 us -> 27.9 us (level)
  no operation moved by 1% of the time
where the time goes in v3:
time: 27.9 us; the launch traced here: 27.8 us
  Pallas kernels  27.1 us (97%)
  local copies, waits for them, and re-layouts  0.71 us (3%)
    pallas_call x1, Pallas kernels, local(): pl.pallas_call(functools.partial(kernel, targets.shape[1]), out_shape=plt...  27.1 us
    unnamed x1, local copies, waits for them, and re-layouts  0.71 us

profile of v3, /device:TPU:1, one launch (start us, length us, event | category | flops | bytes accessed | tf_op | source)
XLA Modules:
  0.0 27.8 jit_solution(9184738354409257562)
XLA Ops:
  0.0 27.1 %shard_map.55 = bf16[1,2,4,128,128]{4,3,2,1,0:T(8,128)(2,1)S(1)} custom-call(bf16[4,4,26]{2,1,0:T(4,128)(2,1)} %bitcast.2, s32[8,26]{1,0:T(8,128)} %bitcast.3, bf16[1,2,4,128,128]{4,3,2,1,0:T(8,128)(2,1)} %psi_hbm.1, bf16[1,26,2,128,128]{4,3,2,1,0:T(8,128)(2,1)} %left_ref.1, bf16[1,26,2,128,128]{4,3,2,1,0:T(8,128)(2,1)} %right_ref.1), custom_call_target="tpu_custom_call" | custom-call | tf_op jit(solution)/shard_map/pallas_call | solution.py:343
  27.1 0.7 %copy.7 = bf16[1,2,4,128,128]{4,3,2,1,0:T(8,128)(2,1)} copy(bf16[1,2,4,128,128]{4,3,2,1,0:T(8,128)(2,1)S(1)} %shard_map.55) | data formatting | bytes 524288
